TPU v7x, 128 devices: a whole 4x4x4 slice. The times are simulated.
128 devices in a mesh: rows: 32 (over y, z_lo, x), tm: 4 (over z_hi, core).
Axes of the slice: x: 4, y: 4, z: 4 (z_hi: 2, z_lo: 2; z = z_hi * 2 + z_lo), core: 2. Of those that a mesh axis runs over, the one named last changes fastest.
Arguments:
- raw_frames: bfloat16 [320, 256, 2048], P('tm', 'rows'), may hold values from -6 to 6
- dark_frame: float32 [256, 2048], P('rows'), may hold values from -0.5 to 0.5
- flat_field: float32 [256, 2048], P('rows'), may hold values from 0.5 to 1.5
- pixel_gain: float32 [256, 2048], P('rows'), may hold values from 0.1 to 1.9
- smoothing_kernel: float32 [5, 5], replicated, may hold values from 0.05 to 0.5
- bin_labels: int32 [256, 2048], P('rows'), may hold values from 0 to 71999
- lag_list: int32 [64], replicated, may hold values from 1 to 79, as said below
Outputs:
- correlation: float32 [4608000], P(('rows', 'tm'))
Inputs may be any that keep to these rules, and one draw needn't show every extreme that they name: `lag_list`: 64 distinct lags in rising order; the first is 1 and the last 79.
All inputs are finite; a program needn't handle non-finite values.
Results may differ from a plain program's by a relative error of at most 0.0054.
Values may be sent and summed in bfloat16 or wider, within the bound.
A program may use at most 256 MiB of HBM per device.

v0:
```python
import jax
import jax.numpy as jnp
from jax import lax
from jax.sharding import PartitionSpec as P

ANG = 360
QB = 200


def padded_2(array, sides, width):
    for axis, dim in sides:
        peers, length = (lax.axis_size(axis), array.shape[dim])
        up = [(i, (i + 1) % peers) for i in range(peers - 1)]
        down = [(j, i) for i, j in up]
        last = lax.slice_in_dim(array, length - width, length, axis=dim)
        initial = lax.slice_in_dim(array, 0, width, axis=dim)
        before = lax.ppermute(last, axis, up)
        after = lax.ppermute(initial, axis, down)
        array = jnp.concatenate([before, array, after], axis=dim)
    return array


def shift_columns(values, offset):
    if offset == 0:
        return values
    zero_pad = jnp.zeros(values.shape[:-1] + (abs(offset),), values.dtype)
    if offset > 0:
        return jnp.concatenate([values[..., offset:], zero_pad], axis=-1)
    return jnp.concatenate([zero_pad, values[..., :offset]], axis=-1)


def smooth_rows(padded, kernel, row_count):
    running = jnp.zeros((padded.shape[0], row_count, padded.shape[2]), jnp.float32)
    for kernel_row in range(5):
        band_rows = padded[:, kernel_row : kernel_row + row_count, :].astype(jnp.float32)
        for kernel_col in range(5):
            running = running + kernel[kernel_row, kernel_col] * shift_columns(
                band_rows, kernel_col - 2
            )
    return running.astype(jnp.bfloat16)


def lag_sums(series, extended, lag_list, divisor):
    frame_span = series.shape[0]
    lag_groups = lag_list.reshape(-1, 8)

    def one_group(lag_group):
        lag_rows = []
        for position in range(8):
            window = lax.dynamic_slice_in_dim(extended, lag_group[position], frame_span, 0)
            lag_rows.append(
                jnp.sum(series.astype(jnp.float32) * window.astype(jnp.float32), axis=0)
            )
        return jnp.stack(lag_rows)

    lagged = lax.map(one_group, lag_groups)
    return lagged.reshape(lag_list.shape[0], -1) / divisor[:, None]


def per_device(
    raw_frames, dark_frame, flat_field, pixel_gain, smoothing_kernel, bin_labels, lag_list
):
    weighted = ((raw_frames.astype(jnp.float32) - dark_frame) * flat_field * pixel_gain).astype(
        jnp.bfloat16
    )
    padded = padded_2(weighted, (("rows", 1),), 2)
    smoothed = smooth_rows(padded, smoothing_kernel, weighted.shape[1])
    block_frames = smoothed.shape[0]
    tm_count = lax.axis_size("tm")
    frame_total = block_frames * tm_count
    divisor = frame_total - lag_list.astype(jnp.float32)
    lag_count = lag_list.shape[0]
    series = lax.all_to_all(smoothed, "tm", split_axis=2, concat_axis=0, tiled=True)
    quarter = series.shape[2]
    labels_here = lax.dynamic_slice_in_dim(bin_labels, lax.axis_index("tm") * quarter, quarter, 1)
    flat_series = series.reshape(series.shape[0], -1)
    tail_zeros = jnp.zeros((block_frames, flat_series.shape[1]), jnp.bfloat16)
    extended = jnp.concatenate([flat_series, tail_zeros], 0)
    lagged = lag_sums(flat_series, extended, lag_list, divisor)
    bin_table = jnp.zeros((lag_count, ANG * QB), jnp.float32)
    bin_table = bin_table.at[:, labels_here.reshape(-1)].add(lagged.reshape(lag_count, -1))
    owned = lax.psum_scatter(bin_table.reshape(-1), ("rows", "tm"), scatter_dimension=0, tiled=True)
    return owned


def solution(mesh):
    return jax.shard_map(
        per_device,
        mesh=mesh,
        in_specs=(
            P("tm", "rows", None),
            P("rows", None),
            P("rows", None),
            P("rows", None),
            P(),
            P("rows", None),
            P(),
        ),
        out_specs=P(("rows", "tm")),
        check_vma=False,
    )
```

profile of v0, /device:TPU:1, one launch (start us, length us, event | category | flops | bytes accessed | tf_op | source)
XLA Modules:
  0.0 744.5 jit_solution(3258186887334234050)
XLA Ops:
  6.5 3.6 multiply_convert_fusion
  10.2 4.0 collective-permute-start
  14.2 1.3 collective-permute-start.1
  15.5 5.3 fusion.27
  20.9 0.7 fusion.29
  22.3 5.4 fusion.28
  27.7 3.8 collective-permute-done.1
  31.5 4.6 fusion.13
  36.1 15.6 %fusion.18 = (f32[80,8,2046]{2,0,1:T(8,128)}, f32[80,8,2046]{2,0,1:T(8,128)}, f32[80,8,2046]{2,0,1:T(8,128)}, f32[80,8,2046]{2,0,1:T(8,128)}) fusion(f32[80,8,2048]{2,0,1:T(8,128)} %get-tuple-element.75, f32[80,8,2048]{2,0,1:T(8,128)} %get-tuple-element.76), kind=kLoop, calls=%fused_computation.41 | loop fusion | bytes 41902080 | tf_op jit(solution)/shard_map/slice | solution.py:29
  51.7 15.7 %fusion.19 = (f32[80,8,2047]{2,0,1:T(8,128)}, f32[80,8,2047]{2,0,1:T(8,128)}, f32[80,8,2047]{2,0,1:T(8,128)}, f32[80,8,2047]{2,0,1:T(8,128)}) fusion(f32[80,8,2048]{2,0,1:T(8,128)} %get-tuple-element.75, f32[80,8,2048]{2,0,1:T(8,128)} %get-tuple-element.76), kind=kLoop, calls=%fused_computation.42 | loop fusion | bytes 41922560 | tf_op jit(solution)/shard_map/slice | solution.py:29
  67.4 8.5 %fusion.23 = (f32[80,8,2047]{2,0,1:T(8,128)}, f32[80,8,2047]{2,0,1:T(8,128)}, f32[80,8,2047]{2,0,1:T(8,128)}, f32[80,8,2047]{2,0,1:T(8,128)}) fusion(f32[80,8,2048]{2,0,1:T(8,128)S(1)} %get-tuple-element.80, f32[80,8,2048]{2,0,1:T(8,128)S(1)} %get-tuple-element.79), kind=kLoop, calls=%fused_computation.46 | loop fusion | bytes 41922560 | tf_op jit(solution)/shard_map/slice | solution.py:29
  75.9 8.5 %fusion.22 = (f32[80,8,2046]{2,0,1:T(8,128)}, f32[80,8,2046]{2,0,1:T(8,128)}, f32[80,8,2046]{2,0,1:T(8,128)}, f32[80,8,2046]{2,0,1:T(8,128)}) fusion(f32[80,8,2048]{2,0,1:T(8,128)S(1)} %get-tuple-element.80, f32[80,8,2048]{2,0,1:T(8,128)S(1)} %get-tuple-element.79), kind=kLoop, calls=%fused_computation.45 | loop fusion | bytes 41902080 | tf_op jit(solution)/shard_map/slice | solution.py:29
  84.4 50.3 %add_convert_fusion = bf16[80,8,2048]{2,0,1:T(8,128)(2,1)} fusion(f32[80,8,2046]{2,0,1:T(8,128)} %get-tuple-element.116, f32[80,8,2047]{2,0,1:T(8,128)} %get-tuple-element.118, f32[80,8,2047]{2,0,1:T(8,128)} %get-tuple-element.119, f32[80,8,2046]{2,0,1:T(8,128)} %get-tuple-element.117, f32[80,8,2046]{2,0,1:T(8,128)} %get-tuple-element.68, ...), kind=kLoop, calls=%fused_computation.21 | loop fusion | flops 77332480 | bytes 111334496 | tf_op jit(solution)/shard_map/convert_element_type | solution.py:40
  134.6 6.2 copy.24
  140.9 7.1 all-to-all-start
  149.3 47.4 %all-to-all-done = bf16[80,8,2048]{0,1,2:T(8,128)(2,1)} async-done(((bf16[80,8,2048]{0,1,2:T(8,128)(2,1)}), bf16[80,8,2048]{0,1,2:T(8,128)(2,1)}, u32[]{:S(2)}, u32[]{:S(2)}) %all-to-all-start) | async-done | bytes 2621472 | tf_op jit(solution)/shard_map/all_to_all | solution.py:73
  196.7 6.7 copy.25
  203.4 1.2 copy.29
  204.9 1.1 copy-done.2
  206.1 215.6 %while.10 = (s32[]{:T(128)}, f32[8,8,4096]{2,1,0:T(8,128)}, bf16[320,4096]{1,0:T(8,128)(2,1)}, s32[8,8]{1,0:T(8,128)}, bf16[400,4096]{1,0:T(8,128)(2,1)S(1)}, /*index=5*/s32[]{:T(128)}, s32[]{:T(128)}, s32[]{:T(128)}) while((s32[]{:T(128)}, f32[8,8,4096]{2,1,0:T(8,128)}, bf16[320,4096]{1,0:T(8,128)(2,1)}, s32[8,8]{1,0:T(8,128)}, ...), condition=%wide.region_9.10_spmd, body=%wide.region_0.9_spmd.sunk | while | flops 32735256 | bytes 24249352 | solution.py:56
  206.1 0.7 constant_dynamic-slice_fusion.2
  206.8 0.7 fusion.33
  223.0 9.2 %fusion.34 = (f32[4096]{0:T(1024)S(1)}, f32[4096]{0:T(1024)S(1)}, f32[4096]{0:T(1024)S(1)}, f32[4096]{0:T(1024)S(1)}, f32[4096]{0:T(1024)S(1)}, /*index=5*/f32[4096]{0:T(1024)S(1)}, f32[4096]{0:T(1024)S(1)}, f32[4096]{0:T(1024)S(1)}) fusion(bf16[320,4096]{1,0:T(8,128)(2,1)} %get-tuple-element.201, bf16[400,4096]{1,0:T(8,128)(2,1)S(1)} %get-tuple-element.203, ...), kind=kLoop, calls=%fused_computation.16.clone.1 | loop fusion | flops 32735232 | bytes 23724064 | tf_op jit(solution)/shard_map/while/body/eval_jaxpr/reduce_sum | solution.py:52
  233.0 0.7 constant_dynamic-slice_fusion.2
  233.7 0.7 fusion.33
  250.0 9.2 %fusion.34 = (f32[4096]{0:T(1024)S(1)}, f32[4096]{0:T(1024)S(1)}, f32[4096]{0:T(1024)S(1)}, f32[4096]{0:T(1024)S(1)}, f32[4096]{0:T(1024)S(1)}, /*index=5*/f32[4096]{0:T(1024)S(1)}, f32[4096]{0:T(1024)S(1)}, f32[4096]{0:T(1024)S(1)}) fusion(bf16[320,4096]{1,0:T(8,128)(2,1)} %get-tuple-element.201, bf16[400,4096]{1,0:T(8,128)(2,1)S(1)} %get-tuple-element.203, ...), kind=kLoop, calls=%fused_computation.16.clone.1 | loop fusion | flops 32735232 | bytes 23724064 | tf_op jit(solution)/shard_map/while/body/eval_jaxpr/reduce_sum | solution.py:52
  260.0 0.7 constant_dynamic-slice_fusion.2
  260.7 0.7 fusion.33
  276.9 9.2 %fusion.34 = (f32[4096]{0:T(1024)S(1)}, f32[4096]{0:T(1024)S(1)}, f32[4096]{0:T(1024)S(1)}, f32[4096]{0:T(1024)S(1)}, f32[4096]{0:T(1024)S(1)}, /*index=5*/f32[4096]{0:T(1024)S(1)}, f32[4096]{0:T(1024)S(1)}, f32[4096]{0:T(1024)S(1)}) fusion(bf16[320,4096]{1,0:T(8,128)(2,1)} %get-tuple-element.201, bf16[400,4096]{1,0:T(8,128)(2,1)S(1)} %get-tuple-element.203, ...), kind=kLoop, calls=%fused_computation.16.clone.1 | loop fusion | flops 32735232 | bytes 23724064 | tf_op jit(solution)/shard_map/while/body/eval_jaxpr/reduce_sum | solution.py:52
  286.9 0.7 constant_dynamic-slice_fusion.2
  287.6 0.7 fusion.33
  303.8 9.2 %fusion.34 = (f32[4096]{0:T(1024)S(1)}, f32[4096]{0:T(1024)S(1)}, f32[4096]{0:T(1024)S(1)}, f32[4096]{0:T(1024)S(1)}, f32[4096]{0:T(1024)S(1)}, /*index=5*/f32[4096]{0:T(1024)S(1)}, f32[4096]{0:T(1024)S(1)}, f32[4096]{0:T(1024)S(1)}) fusion(bf16[320,4096]{1,0:T(8,128)(2,1)} %get-tuple-element.201, bf16[400,4096]{1,0:T(8,128)(2,1)S(1)} %get-tuple-element.203, ...), kind=kLoop, calls=%fused_computation.16.clone.1 | loop fusion | flops 32735232 | bytes 23724064 | tf_op jit(solution)/shard_map/while/body/eval_jaxpr/reduce_sum | solution.py:52
  313.9 0.7 constant_dynamic-slice_fusion.2
  314.5 0.7 fusion.33
  330.8 9.2 %fusion.34 = (f32[4096]{0:T(1024)S(1)}, f32[4096]{0:T(1024)S(1)}, f32[4096]{0:T(1024)S(1)}, f32[4096]{0:T(1024)S(1)}, f32[4096]{0:T(1024)S(1)}, /*index=5*/f32[4096]{0:T(1024)S(1)}, f32[4096]{0:T(1024)S(1)}, f32[4096]{0:T(1024)S(1)}) fusion(bf16[320,4096]{1,0:T(8,128)(2,1)} %get-tuple-element.201, bf16[400,4096]{1,0:T(8,128)(2,1)S(1)} %get-tuple-element.203, ...), kind=kLoop, calls=%fused_computation.16.clone.1 | loop fusion | flops 32735232 | bytes 23724064 | tf_op jit(solution)/shard_map/while/body/eval_jaxpr/reduce_sum | solution.py:52
  340.8 0.7 constant_dynamic-slice_fusion.2
  341.5 0.7 fusion.33
  357.7 9.2 %fusion.34 = (f32[4096]{0:T(1024)S(1)}, f32[4096]{0:T(1024)S(1)}, f32[4096]{0:T(1024)S(1)}, f32[4096]{0:T(1024)S(1)}, f32[4096]{0:T(1024)S(1)}, /*index=5*/f32[4096]{0:T(1024)S(1)}, f32[4096]{0:T(1024)S(1)}, f32[4096]{0:T(1024)S(1)}) fusion(bf16[320,4096]{1,0:T(8,128)(2,1)} %get-tuple-element.201, bf16[400,4096]{1,0:T(8,128)(2,1)S(1)} %get-tuple-element.203, ...), kind=kLoop, calls=%fused_computation.16.clone.1 | loop fusion | flops 32735232 | bytes 23724064 | tf_op jit(solution)/shard_map/while/body/eval_jaxpr/reduce_sum | solution.py:52
  367.8 0.7 constant_dynamic-slice_fusion.2
  384.7 9.2 %fusion.34 = (f32[4096]{0:T(1024)S(1)}, f32[4096]{0:T(1024)S(1)}, f32[4096]{0:T(1024)S(1)}, f32[4096]{0:T(1024)S(1)}, f32[4096]{0:T(1024)S(1)}, /*index=5*/f32[4096]{0:T(1024)S(1)}, f32[4096]{0:T(1024)S(1)}, f32[4096]{0:T(1024)S(1)}) fusion(bf16[320,4096]{1,0:T(8,128)(2,1)} %get-tuple-element.201, bf16[400,4096]{1,0:T(8,128)(2,1)S(1)} %get-tuple-element.203, ...), kind=kLoop, calls=%fused_computation.16.clone.1 | loop fusion | flops 32735232 | bytes 23724064 | tf_op jit(solution)/shard_map/while/body/eval_jaxpr/reduce_sum | solution.py:52
  394.7 0.7 constant_dynamic-slice_fusion.2
  411.6 9.2 %fusion.34 = (f32[4096]{0:T(1024)S(1)}, f32[4096]{0:T(1024)S(1)}, f32[4096]{0:T(1024)S(1)}, f32[4096]{0:T(1024)S(1)}, f32[4096]{0:T(1024)S(1)}, /*index=5*/f32[4096]{0:T(1024)S(1)}, f32[4096]{0:T(1024)S(1)}, f32[4096]{0:T(1024)S(1)}) fusion(bf16[320,4096]{1,0:T(8,128)(2,1)} %get-tuple-element.201, bf16[400,4096]{1,0:T(8,128)(2,1)S(1)} %get-tuple-element.203, ...), kind=kLoop, calls=%fused_computation.16.clone.1 | loop fusion | flops 32735232 | bytes 23724064 | tf_op jit(solution)/shard_map/while/body/eval_jaxpr/reduce_sum | solution.py:52
  421.7 1.4 fusion.16
  423.6 36.8 %scatter_custom_fusion = f32[64,72000]{0,1:T(8,128)} fusion(s32[4096]{0:T(1024)S(1)} %bitcast.107, f32[4096,64]{1,0:T(8,128)S(1)} %copy.26, f32[]{:T(128)} %constant.3.clone.1), kind=kCustom, calls=%fused_computation.19 | custom fusion | flops 262144 | bytes 18432004 | tf_op jit(solution)/shard_map/scatter-add | solution.py:81
  460.5 27.3 %copy.27 = f32[64,72000]{1,0:T(8,128)} copy(f32[64,72000]{0,1:T(8,128)} %scatter_custom_fusion) | data formatting | bytes 36864000 | tf_op jit(solution)/shard_map/scatter-add | solution.py:81
  487.8 26.6 %reshape.68 = f32[4608000]{0:T(1024)} reshape(f32[64,72000]{1,0:T(8,128)} %copy.27) | data formatting | bytes 36864000 | tf_op jit(solution)/shard_map/reshape | solution.py:82
  514.4 221.5 %all-reduce.24.cloned.1.call-done = f32[4608000]{0:T(1024)} async-done(((f32[4608000]{0:T(1024)}), f32[4608000]{0:T(1024)}) %all-reduce.24.cloned.1.call-update) | async-done | bytes 18432016
  736.0 1.7 dynamic-slice
  (42 shorter events, 11.3 us)
Async XLA Ops:
  6.5 142.1 %copy-start = (s32[8,2048]{1,0:T(8,128)S(1)}, s32[8,2048]{1,0:T(8,128)}, u32[]{:S(2)}) copy-start(s32[8,2048]{1,0:T(8,128)} %param.14) | copy-start | bytes 196612
  10.2 17.4 %collective-permute-start = (bf16[80,2,2048]{2,0,1:T(8,128)(2,1)S(1)}, bf16[80,2,2048]{2,0,1:T(8,128)(2,1)S(1)}, u32[]{:S(2)}, u32[]{:S(2)}) collective-permute-start(bf16[80,2,2048]{2,0,1:T(8,128)(2,1)S(1)} %get-tuple-element.81), channel_id=1, source_target_pairs={{0,4},{4,8},{8,12},{12,16},{16,20},{20,24},{24,28},{28,32},{32,36}... | collective-permute-start | bytes 1966088 | tf_op jit(solution)/shard_map/ppermute | solution.py:17
  14.2 6.7 copy-start.4
  14.2 17.2 %collective-permute-start.1 = (bf16[80,2,2048]{2,0,1:T(8,128)(2,1)S(1)}, bf16[80,2,2048]{2,0,1:T(8,128)(2,1)S(1)}, u32[]{:S(2)}, u32[]{:S(2)}) collective-permute-start(bf16[80,2,2048]{2,0,1:T(8,128)(2,1)S(1)} %get-tuple-element.82), channel_id=1, source_target_pairs={{4,0},{8,4},{12,8},{16,12},{20,16},{24,20},{28,24},{32,28},{36,32}... | collective-permute-start | bytes 1966088 | tf_op jit(solution)/shard_map/ppermute | solution.py:18
  31.5 4.6 copy-start.3
  140.9 7.1 copy-start.5
  140.9 55.8 %all-to-all-start = ((bf16[80,8,2048]{0,1,2:T(8,128)(2,1)}), bf16[80,8,2048]{0,1,2:T(8,128)(2,1)}, u32[]{:S(2)}, u32[]{:S(2)}) async-start(bf16[80,8,2048]{0,1,2:T(8,128)(2,1)} %copy.24), calls=%async_computation | async-start | bytes 8388608 | tf_op jit(solution)/shard_map/all_to_all | solution.py:73
  148.0 588.0 %all-reduce.24.cloned.1.call-start = ((), (), s32[]{:S(2)}) async-start(), calls=%async_computation.1 | async-start | bytes 36864000
  204.6 1.5 copy-start.2
  514.4 223.2 %copy-start.1 = (s32[8,2048]{1,0:T(8,128)S(1)}, s32[8,2048]{1,0:T(8,128)}, u32[]{:S(2)}) copy-start(s32[8,2048]{1,0:T(8,128)} %param.14) | copy-start | bytes 196612
Sparse Core Ops, SparseCore 0:
  514.6 221.3 all-reduce.23
where the time goes:
time: 748 us; the launch traced here: 744 us
  waiting for transfers between devices  273 us (36%)
  other arithmetic  170 us (23%)
  local copies, waits for them, and re-layouts  151 us (20%)
  loops' own time  124 us (17%)
  between operations  13.5 us (2%)
  starting transfers between devices  12.4 us (2%)
    unnamed x2, waiting for transfers between devices  222 us
    another operation x1, loops' own time, lag_sums(): lagged = lax.map(one_group, lag_groups)  124 us
    reduce_sum x8, other arithmetic, one_group(): jnp.sum(series.astype(jnp.float32) * window.astype(jnp.float32), axis=0)  73.2 us
    slice x6, local copies, waits for them, and re-layouts, shift_columns(): return jnp.concatenate([zero_pad, values[..., :offset]], axis=-1)  59 us
    convert_element_type x1, other arithmetic, smooth_rows(): return running.astype(jnp.bfloat16)  50.3 us
    all_to_all x1, waiting for transfers between devices, per_device(): lax.all_to_all(smoothed, 'tm', split_axis=2, concat_axis=0, tiled=True)  47.4 us
    scatter-add x1, other arithmetic, per_device(): bin_table.at[:, labels_here.reshape(-1)].add(lagged.reshape(lag_count, -1))  36.8 us
    scatter-add x1, local copies, waits for them, and re-layouts, per_device(): bin_table.at[:, labels_here.reshape(-1)].add(lagged.reshape(lag_count, -1))  27.3 us
  transfers between devices with their start and end apart: 4, of which 3 were waited for; matrix products, arithmetic and copies ran while one was open for 2% of the time, Pallas kernels for 0%

commit v1 on v0

--- a/solution.py
+++ b/solution.py
@@ -70,7 +70,10 @@
     frame_total = block_frames * tm_count
     divisor = frame_total - lag_list.astype(jnp.float32)
     lag_count = lag_list.shape[0]
-    series = lax.all_to_all(smoothed, "tm", split_axis=2, concat_axis=0, tiled=True)
+    size = lax.axis_size("tm")
+    blocks = jnp.stack(jnp.split(smoothed, size, axis=2), axis=0)
+    blocks = lax.all_to_all(blocks, "tm", split_axis=0, concat_axis=0)
+    series = jnp.concatenate(blocks, axis=0)
     quarter = series.shape[2]
     labels_here = lax.dynamic_slice_in_dim(bin_labels, lax.axis_index("tm") * quarter, quarter, 1)
     flat_series = series.reshape(series.shape[0], -1)

time: 748 us -> 718 us (0.960)
  waiting for transfers between devices: 273 us -> 256 us
  local copies, waits for them, and re-layouts: 151 us -> 141 us
    all_to_all x1, waiting for transfers between devices: 47.4 us -> 30.6 us  [per_device(): blocks = lax.all_to_all(blocks, 'tm', split_axis=0, concat_axis=0)]
where the time goes in v1:
time: 718 us; the launch traced here: 715 us
  waiting for transfers between devices  256 us (36%)
  other arithmetic  172 us (24%)
  local copies, waits for them, and re-layouts  141 us (20%)
  loops' own time  120 us (17%)
  between operations  13.5 us (2%)
  starting transfers between devices  12.2 us (2%)
    unnamed x2, waiting for transfers between devices  221 us
    another operation x1, loops' own time, lag_sums(): lagged = lax.map(one_group, lag_groups)  120 us
    reduce_sum x8, other arithmetic, one_group(): jnp.sum(series.astype(jnp.float32) * window.astype(jnp.float32), axis=0)  73.2 us
    slice x6, local copies, waits for them, and re-layouts, shift_columns(): return jnp.concatenate([zero_pad, values[..., :offset]], axis=-1)  59 us
    convert_element_type x1, other arithmetic, smooth_rows(): return running.astype(jnp.bfloat16)  50.3 us
    scatter-add x1, other arithmetic, per_device(): bin_table.at[:, labels_here.reshape(-1)].add(lagged.reshape(lag_count, -1))  36.8 us
    all_to_all x1, waiting for transfers between devices, per_device(): blocks = lax.all_to_all(blocks, 'tm', split_axis=0, concat_axis=0)  30.6 us
    scatter-add x1, local copies, waits for them, and re-layouts, per_device(): bin_table.at[:, labels_here.reshape(-1)].add(lagged.reshape(lag_count, -1))  27.3 us
  transfers between devices with their start and end apart: 4, of which 3 were waited for; matrix products, arithmetic and copies ran while one was open for 2% of the time, Pallas kernels for 0%

profile of v1, /device:TPU:1, one launch (start us, length us, event | category | flops | bytes accessed | tf_op | source)
XLA Modules:
  0.0 714.6 jit_solution(4539091246216077780)
XLA Ops:
  6.5 3.6 multiply_convert_fusion
  10.2 4.0 collective-permute-start
  14.2 1.3 collective-permute-start.1
  15.5 5.3 fusion.27
  20.9 0.7 fusion.29
  22.3 5.4 fusion.28
  27.7 3.8 collective-permute-done.1
  31.5 4.6 fusion.13
  36.1 15.6 %fusion.18 = (f32[80,8,2046]{2,0,1:T(8,128)}, f32[80,8,2046]{2,0,1:T(8,128)}, f32[80,8,2046]{2,0,1:T(8,128)}, f32[80,8,2046]{2,0,1:T(8,128)}) fusion(f32[80,8,2048]{2,0,1:T(8,128)} %get-tuple-element.75, f32[80,8,2048]{2,0,1:T(8,128)} %get-tuple-element.76), kind=kLoop, calls=%fused_computation.46 | loop fusion | bytes 41902080 | tf_op jit(solution)/shard_map/slice | solution.py:29
  51.7 15.7 %fusion.19 = (f32[80,8,2047]{2,0,1:T(8,128)}, f32[80,8,2047]{2,0,1:T(8,128)}, f32[80,8,2047]{2,0,1:T(8,128)}, f32[80,8,2047]{2,0,1:T(8,128)}) fusion(f32[80,8,2048]{2,0,1:T(8,128)} %get-tuple-element.75, f32[80,8,2048]{2,0,1:T(8,128)} %get-tuple-element.76), kind=kLoop, calls=%fused_computation.47 | loop fusion | bytes 41922560 | tf_op jit(solution)/shard_map/slice | solution.py:29
  67.4 8.5 %fusion.23 = (f32[80,8,2047]{2,0,1:T(8,128)}, f32[80,8,2047]{2,0,1:T(8,128)}, f32[80,8,2047]{2,0,1:T(8,128)}, f32[80,8,2047]{2,0,1:T(8,128)}) fusion(f32[80,8,2048]{2,0,1:T(8,128)S(1)} %get-tuple-element.84, f32[80,8,2048]{2,0,1:T(8,128)S(1)} %get-tuple-element.83), kind=kLoop, calls=%fused_computation.51 | loop fusion | bytes 41922560 | tf_op jit(solution)/shard_map/slice | solution.py:29
  75.9 8.5 %fusion.22 = (f32[80,8,2046]{2,0,1:T(8,128)}, f32[80,8,2046]{2,0,1:T(8,128)}, f32[80,8,2046]{2,0,1:T(8,128)}, f32[80,8,2046]{2,0,1:T(8,128)}) fusion(f32[80,8,2048]{2,0,1:T(8,128)S(1)} %get-tuple-element.84, f32[80,8,2048]{2,0,1:T(8,128)S(1)} %get-tuple-element.83), kind=kLoop, calls=%fused_computation.50 | loop fusion | bytes 41902080 | tf_op jit(solution)/shard_map/slice | solution.py:29
  84.4 50.3 %add_convert_fusion = bf16[80,8,2048]{2,0,1:T(8,128)(2,1)} fusion(f32[80,8,2046]{2,0,1:T(8,128)} %get-tuple-element.120, f32[80,8,2047]{2,0,1:T(8,128)} %get-tuple-element.122, f32[80,8,2047]{2,0,1:T(8,128)} %get-tuple-element.123, f32[80,8,2046]{2,0,1:T(8,128)} %get-tuple-element.121, f32[80,8,2046]{2,0,1:T(8,128)} %get-tuple-element.68, ...), kind=kLoop, calls=%fused_computation.21 | loop fusion | flops 77332480 | bytes 111334496 | tf_op jit(solution)/shard_map/convert_element_type | solution.py:40
  134.6 1.9 slice_bitcast_fusion.3
  136.5 1.8 pad_maximum_fusion.2
  138.3 7.0 all-to-all-start
  146.5 30.6 %all-to-all-done = bf16[4,80,8,512]{3,1,2,0:T(8,128)(2,1)S(1)} async-done(((bf16[4,80,8,512]{3,1,2,0:T(8,128)(2,1)}), bf16[4,80,8,512]{3,1,2,0:T(8,128)(2,1)S(1)}, u32[]{:S(2)}, u32[]{:S(2)}) %all-to-all-start) | async-done | bytes 2621472 | tf_op jit(solution)/shard_map/all_to_all | solution.py:75
  177.1 1.5 copy.19
  178.6 1.2 copy.23
  180.2 1.1 copy-done.2
  181.3 210.8 %while.10 = (s32[]{:T(128)}, f32[8,8,4096]{2,1,0:T(8,128)}, bf16[320,4096]{1,0:T(8,128)(2,1)}, s32[8,8]{1,0:T(8,128)}, bf16[400,4096]{1,0:T(8,128)(2,1)S(1)}, /*index=5*/s32[]{:T(128)}, s32[]{:T(128)}, s32[]{:T(128)}) while((s32[]{:T(128)}, f32[8,8,4096]{2,1,0:T(8,128)}, bf16[320,4096]{1,0:T(8,128)(2,1)}, s32[8,8]{1,0:T(8,128)}, ...), condition=%wide.region_9.10_spmd, body=%wide.region_0.9_spmd.sunk | while | flops 32735256 | bytes 24249352 | solution.py:56
  181.3 0.7 constant_dynamic-slice_fusion.2
  182.0 0.7 fusion.33
  197.6 9.2 %fusion.34 = (f32[4096]{0:T(1024)S(1)}, f32[4096]{0:T(1024)S(1)}, f32[4096]{0:T(1024)S(1)}, f32[4096]{0:T(1024)S(1)}, f32[4096]{0:T(1024)S(1)}, /*index=5*/f32[4096]{0:T(1024)S(1)}, f32[4096]{0:T(1024)S(1)}, f32[4096]{0:T(1024)S(1)}) fusion(bf16[320,4096]{1,0:T(8,128)(2,1)} %get-tuple-element.205, bf16[400,4096]{1,0:T(8,128)(2,1)S(1)} %get-tuple-element.207, ...), kind=kLoop, calls=%fused_computation.16.clone.1 | loop fusion | flops 32735232 | bytes 23724064 | tf_op jit(solution)/shard_map/while/body/eval_jaxpr/reduce_sum | solution.py:52
  207.7 0.7 constant_dynamic-slice_fusion.2
  208.3 0.7 fusion.33
  224.0 9.2 %fusion.34 = (f32[4096]{0:T(1024)S(1)}, f32[4096]{0:T(1024)S(1)}, f32[4096]{0:T(1024)S(1)}, f32[4096]{0:T(1024)S(1)}, f32[4096]{0:T(1024)S(1)}, /*index=5*/f32[4096]{0:T(1024)S(1)}, f32[4096]{0:T(1024)S(1)}, f32[4096]{0:T(1024)S(1)}) fusion(bf16[320,4096]{1,0:T(8,128)(2,1)} %get-tuple-element.205, bf16[400,4096]{1,0:T(8,128)(2,1)S(1)} %get-tuple-element.207, ...), kind=kLoop, calls=%fused_computation.16.clone.1 | loop fusion | flops 32735232 | bytes 23724064 | tf_op jit(solution)/shard_map/while/body/eval_jaxpr/reduce_sum | solution.py:52
  234.0 0.7 constant_dynamic-slice_fusion.2
  234.7 0.7 fusion.33
  250.3 9.2 %fusion.34 = (f32[4096]{0:T(1024)S(1)}, f32[4096]{0:T(1024)S(1)}, f32[4096]{0:T(1024)S(1)}, f32[4096]{0:T(1024)S(1)}, f32[4096]{0:T(1024)S(1)}, /*index=5*/f32[4096]{0:T(1024)S(1)}, f32[4096]{0:T(1024)S(1)}, f32[4096]{0:T(1024)S(1)}) fusion(bf16[320,4096]{1,0:T(8,128)(2,1)} %get-tuple-element.205, bf16[400,4096]{1,0:T(8,128)(2,1)S(1)} %get-tuple-element.207, ...), kind=kLoop, calls=%fused_computation.16.clone.1 | loop fusion | flops 32735232 | bytes 23724064 | tf_op jit(solution)/shard_map/while/body/eval_jaxpr/reduce_sum | solution.py:52
  260.4 0.7 constant_dynamic-slice_fusion.2
  261.1 0.7 fusion.33
  276.7 9.2 %fusion.34 = (f32[4096]{0:T(1024)S(1)}, f32[4096]{0:T(1024)S(1)}, f32[4096]{0:T(1024)S(1)}, f32[4096]{0:T(1024)S(1)}, f32[4096]{0:T(1024)S(1)}, /*index=5*/f32[4096]{0:T(1024)S(1)}, f32[4096]{0:T(1024)S(1)}, f32[4096]{0:T(1024)S(1)}) fusion(bf16[320,4096]{1,0:T(8,128)(2,1)} %get-tuple-element.205, bf16[400,4096]{1,0:T(8,128)(2,1)S(1)} %get-tuple-element.207, ...), kind=kLoop, calls=%fused_computation.16.clone.1 | loop fusion | flops 32735232 | bytes 23724064 | tf_op jit(solution)/shard_map/while/body/eval_jaxpr/reduce_sum | solution.py:52
  286.7 0.7 constant_dynamic-slice_fusion.2
  303.1 9.2 %fusion.34 = (f32[4096]{0:T(1024)S(1)}, f32[4096]{0:T(1024)S(1)}, f32[4096]{0:T(1024)S(1)}, f32[4096]{0:T(1024)S(1)}, f32[4096]{0:T(1024)S(1)}, /*index=5*/f32[4096]{0:T(1024)S(1)}, f32[4096]{0:T(1024)S(1)}, f32[4096]{0:T(1024)S(1)}) fusion(bf16[320,4096]{1,0:T(8,128)(2,1)} %get-tuple-element.205, bf16[400,4096]{1,0:T(8,128)(2,1)S(1)} %get-tuple-element.207, ...), kind=kLoop, calls=%fused_computation.16.clone.1 | loop fusion | flops 32735232 | bytes 23724064 | tf_op jit(solution)/shard_map/while/body/eval_jaxpr/reduce_sum | solution.py:52
  313.1 0.7 constant_dynamic-slice_fusion.2
  329.4 9.2 %fusion.34 = (f32[4096]{0:T(1024)S(1)}, f32[4096]{0:T(1024)S(1)}, f32[4096]{0:T(1024)S(1)}, f32[4096]{0:T(1024)S(1)}, f32[4096]{0:T(1024)S(1)}, /*index=5*/f32[4096]{0:T(1024)S(1)}, f32[4096]{0:T(1024)S(1)}, f32[4096]{0:T(1024)S(1)}) fusion(bf16[320,4096]{1,0:T(8,128)(2,1)} %get-tuple-element.205, bf16[400,4096]{1,0:T(8,128)(2,1)S(1)} %get-tuple-element.207, ...), kind=kLoop, calls=%fused_computation.16.clone.1 | loop fusion | flops 32735232 | bytes 23724064 | tf_op jit(solution)/shard_map/while/body/eval_jaxpr/reduce_sum | solution.py:52
  339.4 0.7 constant_dynamic-slice_fusion.2
  340.1 0.7 fusion.33
  355.8 9.2 %fusion.34 = (f32[4096]{0:T(1024)S(1)}, f32[4096]{0:T(1024)S(1)}, f32[4096]{0:T(1024)S(1)}, f32[4096]{0:T(1024)S(1)}, f32[4096]{0:T(1024)S(1)}, /*index=5*/f32[4096]{0:T(1024)S(1)}, f32[4096]{0:T(1024)S(1)}, f32[4096]{0:T(1024)S(1)}) fusion(bf16[320,4096]{1,0:T(8,128)(2,1)} %get-tuple-element.205, bf16[400,4096]{1,0:T(8,128)(2,1)S(1)} %get-tuple-element.207, ...), kind=kLoop, calls=%fused_computation.16.clone.1 | loop fusion | flops 32735232 | bytes 23724064 | tf_op jit(solution)/shard_map/while/body/eval_jaxpr/reduce_sum | solution.py:52
  365.8 0.7 constant_dynamic-slice_fusion.2
  382.1 9.2 %fusion.34 = (f32[4096]{0:T(1024)S(1)}, f32[4096]{0:T(1024)S(1)}, f32[4096]{0:T(1024)S(1)}, f32[4096]{0:T(1024)S(1)}, f32[4096]{0:T(1024)S(1)}, /*index=5*/f32[4096]{0:T(1024)S(1)}, f32[4096]{0:T(1024)S(1)}, f32[4096]{0:T(1024)S(1)}) fusion(bf16[320,4096]{1,0:T(8,128)(2,1)} %get-tuple-element.205, bf16[400,4096]{1,0:T(8,128)(2,1)S(1)} %get-tuple-element.207, ...), kind=kLoop, calls=%fused_computation.16.clone.1 | loop fusion | flops 32735232 | bytes 23724064 | tf_op jit(solution)/shard_map/while/body/eval_jaxpr/reduce_sum | solution.py:52
  392.1 1.4 fusion.16
  394.1 36.8 %scatter_custom_fusion = f32[64,72000]{0,1:T(8,128)} fusion(s32[4096]{0:T(1024)S(1)} %bitcast.112, f32[4096,64]{1,0:T(8,128)S(1)} %copy.20, f32[]{:T(128)} %constant.3.clone.1), kind=kCustom, calls=%fused_computation.19 | custom fusion | flops 262144 | bytes 18432004 | tf_op jit(solution)/shard_map/scatter-add | solution.py:84
  430.9 27.3 %copy.21 = f32[64,72000]{1,0:T(8,128)} copy(f32[64,72000]{0,1:T(8,128)} %scatter_custom_fusion) | data formatting | bytes 36864000 | tf_op jit(solution)/shard_map/scatter-add | solution.py:84
  458.3 26.6 %reshape.63 = f32[4608000]{0:T(1024)} reshape(f32[64,72000]{1,0:T(8,128)} %copy.21) | data formatting | bytes 36864000 | tf_op jit(solution)/shard_map/reshape | solution.py:85
  484.9 221.1 %all-reduce.24.cloned.1.call-done = f32[4608000]{0:T(1024)} async-done(((f32[4608000]{0:T(1024)}), f32[4608000]{0:T(1024)}) %all-reduce.24.cloned.1.call-update) | async-done | bytes 18432016
  706.0 1.7 dynamic-slice
  (43 shorter events, 12.0 us)
Async XLA Ops:
  6.5 139.4 %copy-start = (s32[8,2048]{1,0:T(8,128)S(1)}, s32[8,2048]{1,0:T(8,128)}, u32[]{:S(2)}) copy-start(s32[8,2048]{1,0:T(8,128)} %param.14) | copy-start | bytes 196612
  10.2 17.4 %collective-permute-start = (bf16[80,2,2048]{2,0,1:T(8,128)(2,1)S(1)}, bf16[80,2,2048]{2,0,1:T(8,128)(2,1)S(1)}, u32[]{:S(2)}, u32[]{:S(2)}) collective-permute-start(bf16[80,2,2048]{2,0,1:T(8,128)(2,1)S(1)} %get-tuple-element.85), channel_id=1, source_target_pairs={{0,4},{4,8},{8,12},{12,16},{16,20},{20,24},{24,28},{28,32},{32,36}... | collective-permute-start | bytes 1966088 | tf_op jit(solution)/shard_map/ppermute | solution.py:17
  14.2 6.7 copy-start.4
  14.2 17.2 %collective-permute-start.1 = (bf16[80,2,2048]{2,0,1:T(8,128)(2,1)S(1)}, bf16[80,2,2048]{2,0,1:T(8,128)(2,1)S(1)}, u32[]{:S(2)}, u32[]{:S(2)}) collective-permute-start(bf16[80,2,2048]{2,0,1:T(8,128)(2,1)S(1)} %get-tuple-element.86), channel_id=1, source_target_pairs={{4,0},{8,4},{12,8},{16,12},{20,16},{24,20},{28,24},{32,28},{36,32}... | collective-permute-start | bytes 1966088 | tf_op jit(solution)/shard_map/ppermute | solution.py:18
  31.5 4.6 copy-start.3
  136.5 8.8 %copy-start.5 = (s32[64]{0:T(128)S(1)}, s32[64]{0:T(128)}, u32[]{:S(2)}) copy-start(s32[64]{0:T(128)} %param.15) | copy-start | bytes 772
  138.3 38.8 %all-to-all-start = ((bf16[4,80,8,512]{3,1,2,0:T(8,128)(2,1)}), bf16[4,80,8,512]{3,1,2,0:T(8,128)(2,1)S(1)}, u32[]{:S(2)}, u32[]{:S(2)}) async-start(bf16[4,80,8,512]{3,1,2,0:T(8,128)(2,1)} %pad_maximum_fusion.2), calls=%async_computation | async-start | bytes 5242880 | tf_op jit(solution)/shard_map/all_to_all | solution.py:75
  145.3 560.7 %all-reduce.24.cloned.1.call-start = ((), (), s32[]{:S(2)}) async-start(), calls=%async_computation.1 | async-start | bytes 36864000
  179.8 1.5 copy-start.2
  484.9 222.8 %copy-start.1 = (s32[8,2048]{1,0:T(8,128)S(1)}, s32[8,2048]{1,0:T(8,128)}, u32[]{:S(2)}) copy-start(s32[8,2048]{1,0:T(8,128)} %param.14) | copy-start | bytes 196612
Sparse Core Ops, SparseCore 0:
  485.0 220.9 all-reduce.23
